TPU v7x, 512 devices: a whole 4x8x8 slice. The times are simulated.
512 devices in a mesh: tile: 64 (over z, x, core), tm: 8 (over y).
Axes of the slice: x: 4, y: 8, z: 8, core: 2. Of those that a mesh axis runs over, the one named last changes fastest.
Arguments:
- data: bfloat16 [8192, 64, 128], P('tile', 'tm'), may hold values from -8 to 8
- send_list: int32 [64, 64, 8], P('tile'), may hold values from 0 to 127
- footprint_slot: int32 [8192, 8], P('tile'), may hold values from 0 to 511, as said below
- footprint: bfloat16 [8192, 8, 128], P('tile'), may hold values from 0 to 0.053955078
- colour: int32 [8192], P('tile'), may hold values from 0 to 3, as said below
- correlation: int32 [8192, 8], P('tile'), may hold values from 0 to 8191, as said below
- correlation_gram: float32 [8192, 8], P('tile'), may hold values from 0.01 to 0.15
- traces_init: float32 [64, 8192], P('tm', 'tile'), may hold values from 0 to 4
Outputs:
- traces: float32 [64, 8192], P('tm', 'tile')
- trace_rms: float32 [8192], P('tile')
Inputs may be any that keep to these rules, and one draw needn't show every extreme that they name: footprint_slot[k, j] names the slot c = footprint_slot[k, j] % 8 in which tile device footprint_slot[k, j] // 8 sends a block to the owner of k, tile device k // 128; the 8 slots of one footprint differ. Each tile device owns exactly a quarter of its 128 components in each colour; every listed neighbour has a colour other than the component's own. `correlation`: the tile axis folds the slab's two halves end to end, so the neighbours of a component owned by tile device d are owned by tile device d - 1, d, d + 1 or (d + 32) modulo 64; entries may repeat.
All inputs are finite; a program needn't handle non-finite values.
Results may differ from a plain program's by a relative error of at most 0.0003.
Values may be sent and summed in bfloat16 or wider, within the bound.
A program may use at most 64 MiB of HBM per device.

v0:
```python
import jax
import jax.numpy as jnp
from jax import lax
from jax.sharding import PartitionSpec as P


def shards(
    data, send_list, footprint_slot, footprint, colour, correlation, correlation_gram, traces_init
):
    tile_count = lax.axis_size("tile")
    tile_here = lax.axis_index("tile")
    comp_count = colour.shape[0]
    quarter = comp_count // 4
    frames_dev = data.shape[1]
    voxels = data.shape[2]
    cap_slots = send_list.shape[2]
    slot_count = tile_count * cap_slots
    blocks_fp = footprint.shape[1]
    listed = correlation.shape[1]
    outgoing = data[send_list[0].reshape(-1)].reshape(tile_count, cap_slots, frames_dev, voxels)
    arrived = lax.all_to_all(outgoing, "tile", split_axis=0, concat_axis=0, tiled=True).reshape(
        slot_count, frames_dev, voxels
    )
    weights32 = footprint.astype(jnp.float32)
    self_gram = jnp.sum(weights32 * weights32, axis=(1, 2))
    comp_block = min(32, comp_count)
    block_total = comp_count // comp_block
    slot_range = jnp.arange(slot_count, dtype=jnp.int32)

    def project(inputs):
        slot_ids, weight_rows = inputs
        one_hot = (slot_ids[:, :, None] == slot_range[None, None, :]).astype(jnp.bfloat16)
        spread = jnp.einsum(
            "kjs,kjv->svk", one_hot, weight_rows, preferred_element_type=jnp.bfloat16
        )
        return jnp.einsum("sfv,svk->fk", arrived, spread, preferred_element_type=jnp.float32)

    pieces = lax.map(
        project,
        (
            footprint_slot.reshape(block_total, comp_block, blocks_fp),
            footprint.reshape(block_total, comp_block, blocks_fp, voxels),
        ),
    )
    projected = jnp.transpose(pieces, (1, 0, 2)).reshape(frames_dev, comp_count)
    ordering = jnp.argsort(colour, stable=True)
    grouped = jnp.argsort(ordering)
    rank_in = grouped % quarter
    proj_group = projected[:, ordering].reshape(frames_dev, 4, quarter)
    gram_group = self_gram[ordering].reshape(4, quarter)
    nb_group = correlation[ordering].reshape(4, quarter, listed)
    weight_group = correlation_gram[ordering].reshape(4, quarter, listed)
    start_group = traces_init[:, ordering].reshape(frames_dev, 4, quarter)
    own_flat = colour * (tile_count * quarter) + tile_here * quarter + rank_in
    table, flat_all = (
        lax.all_gather(start_group, "tile", axis=2, tiled=True),
        lax.all_gather(own_flat, "tile", axis=0, tiled=True),
    )
    span_width = tile_count * quarter
    lookup = flat_all[nb_group]
    fresh_parts = []
    for step_colour in range(4):
        flat_table = table.reshape(frames_dev, 4 * span_width)
        values = jnp.take(flat_table, lookup[step_colour].reshape(-1), axis=1).reshape(
            frames_dev, quarter, listed
        )
        neighbour_sum = jnp.sum(values * weight_group[step_colour][None, :, :], axis=2)
        fresh = jnp.maximum(
            (proj_group[:, step_colour, :] - neighbour_sum) / gram_group[step_colour][None, :], 0.0
        )
        fresh_parts.append(fresh)
        if step_colour + 1 < 4:
            arrived_colour = lax.all_gather(fresh, "tile", axis=1, tiled=True)
            table = table.at[:, step_colour, :].set(arrived_colour)
    final_group = jnp.stack(fresh_parts, axis=1).reshape(frames_dev, comp_count)
    traces = final_group[:, grouped]
    energy_sum = lax.psum(jnp.sum(traces * traces, axis=0), "tm")
    trace_rms = jnp.sqrt(energy_sum / (frames_dev * lax.axis_size("tm")) + 1e-06)
    return (traces, trace_rms)


def solution(mesh):
    placed = (
        P("tile", "tm", None),
        P("tile", None, None),
        P("tile", None),
        P("tile", None, None),
        P("tile"),
        P("tile", None),
        P("tile", None),
        P("tm", "tile"),
    )
    return jax.shard_map(
        shards, mesh=mesh, in_specs=placed, out_specs=(P("tm", "tile"), P("tile")), check_vma=False
    )
```

profile of v0, /device:TPU:8, one launch (start us, length us, event | category | flops | bytes accessed | tf_op | source)
XLA Modules:
  0.0 362.0 jit_solution(10333032754767358957)
XLA Ops:
  1.6 2.4 gather_fusion
  4.0 13.8 %all-to-all-start = ((bf16[64,8,8,128]{3,2,1,0:T(8,128)(2,1)}), bf16[64,8,8,128]{3,2,1,0:T(8,128)(2,1)S(1)}, u32[]{:S(2)}, u32[]{:S(2)}) async-start(bf16[64,8,8,128]{3,2,1,0:T(8,128)(2,1)} %bitcast.2), calls=%async_computation | async-start | bytes 2097152 | tf_op jit(solution)/shard_map/all_to_all | solution.py:21
  18.9 2.5 sort.34
  21.4 2.5 sort.35
  24.2 1.2 gather_fusion.6
  27.7 49.4 %all-gather = s32[64,1,128]{2,1,0:T(1,128)S(1)} all-gather(s32[1,1,128]{2,1,0:T(1,128)S(1)} %get-tuple-element.152), channel_id=1, replica_groups=mesh['tile'=64,'tm'=8] {'tile'}, dimensions={0}, use_global_device_ids=true | all-gather | bytes 33280 | tf_op jit(solution)/shard_map/all_gather | solution.py:57
  77.1 6.1 %gather_fusion.4 = s32[1024]{0:T(1024)S(1)} fusion(s32[8192]{0:T(1024)S(1)} %bitcast.154, s32[1024]{0:T(1024)S(1)} %broadcast_clamp_fusion), kind=kCustom, calls=%fused_computation.8 | custom fusion | bytes 12288 | tf_op jit(solution)/shard_map/gather | solution.py:60
  83.2 54.6 %all_gather.15 = f32[8,4,2048]{0,2,1:T(8,128)} all-gather(f32[8,4,32]{0,2,1:T(8,128)S(1)} %bitcast.173), channel_id=1, replica_groups=mesh['tile'=64,'tm'=8] {'tile'}, dimensions={2}, use_global_device_ids=true | all-gather | bytes 266240 | tf_op jit(solution)/shard_map/all_gather | solution.py:56
  137.8 2.9 gather_fusion.8
  141.1 59.1 %while.14 = (s32[]{:T(128)}, f32[4,8,32]{2,1,0:T(8,128)S(1)}, bf16[4,32,8,128]{3,2,1,0:T(8,128)(2,1)S(1)}, s32[4,32,8]{1,0,2:T(4,128)S(1)}, bf16[512,8,128]{2,1,0:T(8,128)(2,1)S(1)}, /*index=5*/s32[]{:T(128)}) while((s32[]{:T(128)}, f32[4,8,32]{2,1,0:T(8,128)S(1)}, bf16[4,32,8,128]{3,2,1,0:T(8,128)(2,1)S(1)}, ...), condition=%wide.region_1.2_spmd.clone, body=%wide.region_0.0_spmd.clone.sunk | while | flops 67239936 | bytes 17915992 | solution.py:38
  141.2 3.3 convolution_bitcast_fusion.3
  144.4 8.0 %copy.102 = bf16[512,128,32]{1,2,0:T(8,128)(2,1)} copy(bf16[512,128,32]{0,1,2:T(8,128)(2,1)} %convolution_bitcast_fusion.3) | data formatting | bytes 8388608 | tf_op jit(solution)/shard_map/while/body/eval_jaxpr/kjs,kjv->svk/transpose | solution.py:33
  152.5 3.4 fusion.42
  155.9 3.3 convolution_bitcast_fusion.3
  159.2 8.0 %copy.102 = bf16[512,128,32]{1,2,0:T(8,128)(2,1)} copy(bf16[512,128,32]{0,1,2:T(8,128)(2,1)} %convolution_bitcast_fusion.3) | data formatting | bytes 8388608 | tf_op jit(solution)/shard_map/while/body/eval_jaxpr/kjs,kjv->svk/transpose | solution.py:33
  167.2 3.4 fusion.42
  170.7 3.3 convolution_bitcast_fusion.3
  174.0 8.0 %copy.102 = bf16[512,128,32]{1,2,0:T(8,128)(2,1)} copy(bf16[512,128,32]{0,1,2:T(8,128)(2,1)} %convolution_bitcast_fusion.3) | data formatting | bytes 8388608 | tf_op jit(solution)/shard_map/while/body/eval_jaxpr/kjs,kjv->svk/transpose | solution.py:33
  182.0 3.4 fusion.42
  185.5 3.3 convolution_bitcast_fusion.3
  188.8 8.0 %copy.102 = bf16[512,128,32]{1,2,0:T(8,128)(2,1)} copy(bf16[512,128,32]{0,1,2:T(8,128)(2,1)} %convolution_bitcast_fusion.3) | data formatting | bytes 8388608 | tf_op jit(solution)/shard_map/while/body/eval_jaxpr/kjs,kjv->svk/transpose | solution.py:33
  196.8 3.4 fusion.42
  201.1 43.3 %all-gather.1 = f32[64,32,8]{1,2,0:T(8,128)S(1)} all-gather(f32[1,32,8]{1,2,0:T(8,128)S(1)} %copy.88), channel_id=1, replica_groups=mesh['tile'=64,'tm'=8] {'tile'}, dimensions={0}, use_global_device_ids=true | all-gather | bytes 66560 | tf_op jit(solution)/shard_map/all_gather | solution.py:73
  244.8 1.1 constant_dynamic-update-slice_fusion.2
  245.9 2.9 gather_fusion.9
  249.1 42.1 %all-gather.2 = f32[64,32,8]{1,2,0:T(8,128)S(1)} all-gather(f32[1,32,8]{1,2,0:T(8,128)S(1)} %copy.91), channel_id=1, replica_groups=mesh['tile'=64,'tm'=8] {'tile'}, dimensions={0}, use_global_device_ids=true | all-gather | bytes 66560 | tf_op jit(solution)/shard_map/all_gather | solution.py:73
  291.7 1.1 constant_dynamic-update-slice_fusion.1
  292.8 2.9 gather_fusion.10
  296.0 43.1 %all-gather.3 = f32[64,32,8]{1,2,0:T(8,128)S(1)} all-gather(f32[1,32,8]{1,2,0:T(8,128)S(1)} %copy.94), channel_id=1, replica_groups=mesh['tile'=64,'tm'=8] {'tile'}, dimensions={0}, use_global_device_ids=true | all-gather | bytes 66560 | tf_op jit(solution)/shard_map/all_gather | solution.py:73
  339.7 1.1 constant_dynamic-update-slice_fusion
  340.7 2.9 gather_fusion.11
  344.7 16.2 %psum.7 = f32[128]{0:T(128)S(1)} all-reduce(f32[128]{0:T(128)S(1)} %multiply_reduce_fusion.1), channel_id=1, replica_groups=mesh['tile'=64,'tm'=8] {'tm'}, use_global_device_ids=true, to_apply=%region_10.12 | all-reduce | flops 128 | bytes 1024 | tf_op jit(solution)/shard_map/psum | solution.py:77
  (79 shorter events, 10.3 us)
Async XLA Ops:
  0.6 1.0 copy-start
  0.6 17.2 %copy-start.1 = (bf16[128,8,128]{2,1,0:T(8,128)(2,1)S(1)}, bf16[128,8,128]{2,1,0:T(8,128)(2,1)}, u32[]{:S(2)}) copy-start(bf16[128,8,128]{2,1,0:T(8,128)(2,1)} %param.21) | copy-start | bytes 786436
  0.7 18.2 %copy-start.6 = (s32[128]{0:T(128)S(1)}, s32[128]{0:T(128)}, u32[]{:S(2)}) copy-start(s32[128]{0:T(128)} %param.22) | copy-start | bytes 1540
  0.7 23.3 %copy-start.2 = (s32[128,8]{0,1:T(8,128)S(1)}, s32[128,8]{0,1:T(8,128)}, u32[]{:S(2)}) copy-start(s32[128,8]{0,1:T(8,128)} %param.20) | copy-start | bytes 12292
  0.7 23.4 %copy-start.3 = (s32[128,8]{0,1:T(8,128)S(1)}, s32[128,8]{0,1:T(8,128)}, u32[]{:S(2)}) copy-start(s32[128,8]{0,1:T(8,128)} %param.23) | copy-start | bytes 12292
  0.7 25.5 %copy-start.4 = (f32[128,8]{0,1:T(8,128)S(1)}, f32[128,8]{0,1:T(8,128)}, u32[]{:S(2)}) copy-start(f32[128,8]{0,1:T(8,128)} %param.24) | copy-start | bytes 12292
  0.7 26.2 %copy-start.5 = (f32[8,128]{1,0:T(8,128)S(1)}, f32[8,128]{1,0:T(8,128)}, u32[]{:S(2)}) copy-start(f32[8,128]{1,0:T(8,128)} %param.25) | copy-start | bytes 12292
  4.0 137.0 %all-to-all-start = ((bf16[64,8,8,128]{3,2,1,0:T(8,128)(2,1)}), bf16[64,8,8,128]{3,2,1,0:T(8,128)(2,1)S(1)}, u32[]{:S(2)}, u32[]{:S(2)}) async-start(bf16[64,8,8,128]{3,2,1,0:T(8,128)(2,1)} %bitcast.2), calls=%async_computation | async-start | bytes 2097152 | tf_op jit(solution)/shard_map/all_to_all | solution.py:21
where the time goes:
time: 363 us; the launch traced here: 362 us
  blocking collectives  249 us (69%)
  local copies, waits for them, and re-layouts  64.4 us (18%)
  matrix products  26.6 us (7%)
  starting transfers between devices  13.8 us (4%)
  other arithmetic  7.73 us (2%)
    all_gather x3, blocking collectives, shards(): arrived_colour = lax.all_gather(fresh, 'tile', axis=1, tiled=True)  128 us
    all_gather x1, blocking collectives, shards(): lax.all_gather(start_group, 'tile', axis=2, tiled=True)  54.6 us
    all_gather x1, blocking collectives, shards(): lax.all_gather(own_flat, 'tile', axis=0, tiled=True)  49.4 us
    transpose x4, local copies, waits for them, and re-layouts, project(): jnp.einsum('kjs,kjv->svk', one_hot, weight_rows, preferred_element_type=j...  32.1 us
    psum x1, blocking collectives, shards(): energy_sum = lax.psum(jnp.sum(traces * traces, axis=0), 'tm')  16.2 us
    all_to_all x1, starting transfers between devices, shards(): lax.all_to_all(outgoing, 'tile', split_axis=0, concat_axis=0, tiled=True)  13.8 us
    dot_general x4, matrix products, project(): jnp.einsum('sfv,svk->fk', arrived, spread, preferred_element_type=jnp.flo...  13.5 us
    dot_general x4, matrix products, project(): jnp.einsum('kjs,kjv->svk', one_hot, weight_rows, preferred_element_type=j...  13.1 us
  transfers between devices with their start and end apart: 1, of which 0 were waited for; matrix products, arithmetic and copies ran while one was open for 5% of the time, Pallas kernels for 0%

commit v1 on v0

--- a/solution.py
+++ b/solution.py
@@ -53,7 +53,9 @@
     start_group = traces_init[:, ordering].reshape(frames_dev, 4, quarter)
     own_flat = colour * (tile_count * quarter) + tile_here * quarter + rank_in
     table, flat_all = (
-        lax.all_gather(start_group, "tile", axis=2, tiled=True),
+        jnp.concatenate(
+            lax.all_to_all(jnp.stack([start_group] * lax.axis_size("tile")), "tile", 0, 0), axis=2
+        ),
         lax.all_gather(own_flat, "tile", axis=0, tiled=True),
     )
     span_width = tile_count * quarter

time: 363 us -> 338 us (0.931)
  blocking collectives: 249 us -> 186 us
  waiting for transfers between devices: 0.01 us -> 11.8 us
  local copies, waits for them, and re-layouts: 64.4 us -> 75.5 us
  starting transfers between devices: 13.8 us -> 20.5 us
  other arithmetic: 7.73 us -> 11.4 us
    all_gather x1 -> x0, blocking collectives: 54.6 us -> none  [shards(): lax.all_gather(start_group, 'tile', axis=2, tiled=True)]
    all_to_all x0 -> x1, starting transfers between devices: none -> 13.8 us  [shards(): lax.all_to_all(jnp.stack([start_group] * lax.axis_size('tile')), 'tile',...]
    all_to_all x1, waiting for transfers between devices: 0.01 us -> 11.8 us  [shards(): lax.all_to_all(outgoing, 'tile', split_axis=0, concat_axis=0, tiled=True)]
    all_gather x1, blocking collectives: 49.4 us -> 41 us  [shards(): lax.all_gather(own_flat, 'tile', axis=0, tiled=True)]
    all_to_all x1, starting transfers between devices: 13.8 us -> 6.75 us  [shards(): lax.all_to_all(outgoing, 'tile', split_axis=0, concat_axis=0, tiled=True)]
    scatter x3 -> x6, local copies, waits for them, and re-layouts: 3.23 us -> 7.76 us  [shards(): table = table.at[:, step_colour, :].set(arrived_colour)]
    reshape x0 -> x4, local copies, waits for them, and re-layouts: none -> 3.84 us  [shards(): jnp.concatenate(lax.all_to_all(jnp.stack([start_group] * lax.axis_size('t...]
  transfers between devices with their start and end apart: 1 -> 2, of which waited for: 0 -> 1; matrix products, arithmetic and copies ran while one was open for 5% -> 7% of each run, Pallas kernels for 0% -> 0%
where the time goes in v1:
time: 338 us; the launch traced here: 336 us
  blocking collectives  186 us (55%)
  local copies, waits for them, and re-layouts  75.5 us (22%)
  matrix products  29.7 us (9%)
  starting transfers between devices  20.5 us (6%)
  waiting for transfers between devices  11.8 us (3%)
  other arithmetic  11.4 us (3%)
    all_gather x3, blocking collectives, shards(): arrived_colour = lax.all_gather(fresh, 'tile', axis=1, tiled=True)  129 us
    all_gather x1, blocking collectives, shards(): lax.all_gather(own_flat, 'tile', axis=0, tiled=True)  41 us
    transpose x4, local copies, waits for them, and re-layouts, project(): jnp.einsum('kjs,kjv->svk', one_hot, weight_rows, preferred_element_type=j...  31.8 us
    dot_general x4, matrix products, project(): jnp.einsum('kjs,kjv->svk', one_hot, weight_rows, preferred_element_type=j...  16.2 us
    psum x1, blocking collectives, shards(): energy_sum = lax.psum(jnp.sum(traces * traces, axis=0), 'tm')  16.1 us
    all_to_all x1, starting transfers between devices, shards(): lax.all_to_all(jnp.stack([start_group] * lax.axis_size('tile')), 'tile',...  13.8 us
    dot_general x4, matrix products, project(): jnp.einsum('sfv,svk->fk', arrived, spread, preferred_element_type=jnp.flo...  13.5 us
    all_to_all x1, waiting for transfers between devices, shards(): lax.all_to_all(outgoing, 'tile', split_axis=0, concat_axis=0, tiled=True)  11.8 us
  transfers between devices with their start and end apart: 2, of which 1 were waited for; matrix products, arithmetic and copies ran while one was open for 7% of the time, Pallas kernels for 0%

profile of v1, /device:TPU:8, one launch (start us, length us, event | category | flops | bytes accessed | tf_op | source)
XLA Modules:
  0.0 336.2 jit_solution(2289618944838083057)
XLA Ops:
  1.5 3.2 sort.34
  4.7 2.5 sort.35
  9.9 13.8 %all-to-all-start.1 = ((f32[64,1,1024]{2,1,0:T(1,128)}), f32[64,1,1024]{2,1,0:T(1,128)S(1)}, u32[]{:S(2)}, u32[]{:S(2)}) async-start(f32[64,1,1024]{2,1,0:T(1,128)} %reshape.406), calls=%async_computation.1 | async-start | bytes 524288 | tf_op jit(solution)/shard_map/all_to_all | solution.py:57
  31.7 41.0 %all-gather = s32[64,1,128]{2,1,0:T(1,128)S(1)} all-gather(s32[1,1,128]{2,1,0:T(1,128)S(1)} %get-tuple-element.152), channel_id=1, replica_groups=mesh['tile'=64,'tm'=8] {'tile'}, dimensions={0}, use_global_device_ids=true | all-gather | bytes 33280 | tf_op jit(solution)/shard_map/all_gather | solution.py:59
  72.7 6.8 %all-to-all-start = ((bf16[64,8,8,128]{3,2,1,0:T(8,128)(2,1)}), bf16[64,8,8,128]{3,2,1,0:T(8,128)(2,1)S(1)}, u32[]{:S(2)}, u32[]{:S(2)}) async-start(bf16[64,8,8,128]{3,2,1,0:T(8,128)(2,1)} %bitcast.2), calls=%async_computation | async-start | bytes 2097152 | tf_op jit(solution)/shard_map/all_to_all | solution.py:21
  79.4 6.2 %gather_fusion.4 = s32[1024]{0:T(1024)S(1)} fusion(s32[8192]{0:T(1024)S(1)} %bitcast.167, s32[1024]{0:T(1024)S(1)} %broadcast_clamp_fusion), kind=kCustom, calls=%fused_computation.8 | custom fusion | bytes 12288 | tf_op jit(solution)/shard_map/gather | solution.py:62
  89.0 2.7 copy.96
  92.7 2.9 gather_fusion.8
  96.5 11.8 %all-to-all-done = bf16[64,8,8,128]{3,2,1,0:T(8,128)(2,1)S(1)} async-done(((bf16[64,8,8,128]{3,2,1,0:T(8,128)(2,1)}), bf16[64,8,8,128]{3,2,1,0:T(8,128)(2,1)S(1)}, u32[]{:S(2)}, u32[]{:S(2)}) %all-to-all-start) | async-done | bytes 1048608 | tf_op jit(solution)/shard_map/all_to_all | solution.py:21
  108.3 61.9 %while.14 = (s32[]{:T(128)}, f32[4,8,32]{2,1,0:T(8,128)S(1)}, bf16[4,32,8,128]{3,2,1,0:T(8,128)(2,1)}, s32[4,32,8]{1,0,2:T(4,128)S(1)}, bf16[512,8,128]{2,1,0:T(8,128)(2,1)S(1)}, /*index=5*/s32[]{:T(128)}) while((s32[]{:T(128)}, f32[4,8,32]{2,1,0:T(8,128)S(1)}, bf16[4,32,8,128]{3,2,1,0:T(8,128)(2,1)}, s32[4,32,8]{1,0,2:T(4,128)S(1)}, ...), condition=%wide.region_1.2_spmd.clone, body=%wide.region_0.0_spmd.clone.sunk | while | flops 67239936 | bytes 17900632 | solution.py:38
  108.4 4.1 %convolution_bitcast_fusion.3 = bf16[512,128,32]{0,1,2:T(8,128)(2,1)} fusion(s32[32,8]{1,0:T(8,128)S(1)} %copy.112, bf16[4,32,8,128]{3,2,1,0:T(8,128)(2,1)} %get-tuple-element.203, s32[]{:T(128)S(6)} %copy.117), kind=kOutput, calls=%fused_computation.13.clone.1 | convolution fusion | flops 33685504 | bytes 4260868 | tf_op jit(solution)/shard_map/while/body/eval_jaxpr/kjs,kjv->svk/dot_general | solution.py:33
  112.4 8.0 %copy.113 = bf16[512,128,32]{1,2,0:T(8,128)(2,1)} copy(bf16[512,128,32]{0,1,2:T(8,128)(2,1)} %convolution_bitcast_fusion.3) | data formatting | bytes 8388608 | tf_op jit(solution)/shard_map/while/body/eval_jaxpr/kjs,kjv->svk/transpose | solution.py:33
  120.4 3.4 %fusion.42 = f32[4,8,32]{2,1,0:T(8,128)S(1)} fusion(f32[4,8,32]{2,1,0:T(8,128)S(1)} %get-tuple-element.196, s32[]{:T(128)S(6)} %copy.117, bf16[512,128,32]{1,2,0:T(8,128)(2,1)} %copy.113, bf16[512,8,128]{2,1,0:T(8,128)(2,1)S(1)} %get-tuple-element.205), kind=kOutput, calls=%fused_computation.15.clone.1 | convolution fusion | flops 33554432 | bytes 5246980 | tf_op jit(solution)/shard_map/while/body/eval_jaxpr/sfv,svk->fk/dot_general | solution.py:36
  123.9 4.1 %convolution_bitcast_fusion.3 = bf16[512,128,32]{0,1,2:T(8,128)(2,1)} fusion(s32[32,8]{1,0:T(8,128)S(1)} %copy.112, bf16[4,32,8,128]{3,2,1,0:T(8,128)(2,1)} %get-tuple-element.203, s32[]{:T(128)S(6)} %copy.117), kind=kOutput, calls=%fused_computation.13.clone.1 | convolution fusion | flops 33685504 | bytes 4260868 | tf_op jit(solution)/shard_map/while/body/eval_jaxpr/kjs,kjv->svk/dot_general | solution.py:33
  127.9 8.0 %copy.113 = bf16[512,128,32]{1,2,0:T(8,128)(2,1)} copy(bf16[512,128,32]{0,1,2:T(8,128)(2,1)} %convolution_bitcast_fusion.3) | data formatting | bytes 8388608 | tf_op jit(solution)/shard_map/while/body/eval_jaxpr/kjs,kjv->svk/transpose | solution.py:33
  135.9 3.4 %fusion.42 = f32[4,8,32]{2,1,0:T(8,128)S(1)} fusion(f32[4,8,32]{2,1,0:T(8,128)S(1)} %get-tuple-element.196, s32[]{:T(128)S(6)} %copy.117, bf16[512,128,32]{1,2,0:T(8,128)(2,1)} %copy.113, bf16[512,8,128]{2,1,0:T(8,128)(2,1)S(1)} %get-tuple-element.205), kind=kOutput, calls=%fused_computation.15.clone.1 | convolution fusion | flops 33554432 | bytes 5246980 | tf_op jit(solution)/shard_map/while/body/eval_jaxpr/sfv,svk->fk/dot_general | solution.py:36
  139.4 4.1 %convolution_bitcast_fusion.3 = bf16[512,128,32]{0,1,2:T(8,128)(2,1)} fusion(s32[32,8]{1,0:T(8,128)S(1)} %copy.112, bf16[4,32,8,128]{3,2,1,0:T(8,128)(2,1)} %get-tuple-element.203, s32[]{:T(128)S(6)} %copy.117), kind=kOutput, calls=%fused_computation.13.clone.1 | convolution fusion | flops 33685504 | bytes 4260868 | tf_op jit(solution)/shard_map/while/body/eval_jaxpr/kjs,kjv->svk/dot_general | solution.py:33
  143.4 8.0 %copy.113 = bf16[512,128,32]{1,2,0:T(8,128)(2,1)} copy(bf16[512,128,32]{0,1,2:T(8,128)(2,1)} %convolution_bitcast_fusion.3) | data formatting | bytes 8388608 | tf_op jit(solution)/shard_map/while/body/eval_jaxpr/kjs,kjv->svk/transpose | solution.py:33
  151.4 3.4 %fusion.42 = f32[4,8,32]{2,1,0:T(8,128)S(1)} fusion(f32[4,8,32]{2,1,0:T(8,128)S(1)} %get-tuple-element.196, s32[]{:T(128)S(6)} %copy.117, bf16[512,128,32]{1,2,0:T(8,128)(2,1)} %copy.113, bf16[512,8,128]{2,1,0:T(8,128)(2,1)S(1)} %get-tuple-element.205), kind=kOutput, calls=%fused_computation.15.clone.1 | convolution fusion | flops 33554432 | bytes 5246980 | tf_op jit(solution)/shard_map/while/body/eval_jaxpr/sfv,svk->fk/dot_general | solution.py:36
  154.8 4.1 %convolution_bitcast_fusion.3 = bf16[512,128,32]{0,1,2:T(8,128)(2,1)} fusion(s32[32,8]{1,0:T(8,128)S(1)} %copy.112, bf16[4,32,8,128]{3,2,1,0:T(8,128)(2,1)} %get-tuple-element.203, s32[]{:T(128)S(6)} %copy.117), kind=kOutput, calls=%fused_computation.13.clone.1 | convolution fusion | flops 33685504 | bytes 4260868 | tf_op jit(solution)/shard_map/while/body/eval_jaxpr/kjs,kjv->svk/dot_general | solution.py:33
  158.9 8.0 %copy.113 = bf16[512,128,32]{1,2,0:T(8,128)(2,1)} copy(bf16[512,128,32]{0,1,2:T(8,128)(2,1)} %convolution_bitcast_fusion.3) | data formatting | bytes 8388608 | tf_op jit(solution)/shard_map/while/body/eval_jaxpr/kjs,kjv->svk/transpose | solution.py:33
  166.9 3.4 %fusion.42 = f32[4,8,32]{2,1,0:T(8,128)S(1)} fusion(f32[4,8,32]{2,1,0:T(8,128)S(1)} %get-tuple-element.196, s32[]{:T(128)S(6)} %copy.117, bf16[512,128,32]{1,2,0:T(8,128)(2,1)} %copy.113, bf16[512,8,128]{2,1,0:T(8,128)(2,1)S(1)} %get-tuple-element.205), kind=kOutput, calls=%fused_computation.15.clone.1 | convolution fusion | flops 33554432 | bytes 5246980 | tf_op jit(solution)/shard_map/while/body/eval_jaxpr/sfv,svk->fk/dot_general | solution.py:36
  171.1 43.9 %all-gather.1 = f32[64,32,8]{1,2,0:T(8,128)S(1)} all-gather(f32[1,32,8]{1,2,0:T(8,128)S(1)} %copy.99), channel_id=1, replica_groups=mesh['tile'=64,'tm'=8] {'tile'}, dimensions={0}, use_global_device_ids=true | all-gather | bytes 66560 | tf_op jit(solution)/shard_map/all_gather | solution.py:75
  215.2 2.6 copy.101
  217.8 2.9 gather_fusion.9
  221.0 41.8 %all-gather.2 = f32[64,32,8]{1,2,0:T(8,128)S(1)} all-gather(f32[1,32,8]{1,2,0:T(8,128)S(1)} %copy.102), channel_id=1, replica_groups=mesh['tile'=64,'tm'=8] {'tile'}, dimensions={0}, use_global_device_ids=true | all-gather | bytes 66560 | tf_op jit(solution)/shard_map/all_gather | solution.py:75
  263.0 2.6 copy.104
  265.6 2.9 gather_fusion.10
  268.8 43.4 %all-gather.3 = f32[64,32,8]{1,2,0:T(8,128)S(1)} all-gather(f32[1,32,8]{1,2,0:T(8,128)S(1)} %copy.105), channel_id=1, replica_groups=mesh['tile'=64,'tm'=8] {'tile'}, dimensions={0}, use_global_device_ids=true | all-gather | bytes 66560 | tf_op jit(solution)/shard_map/all_gather | solution.py:75
  312.4 2.6 copy.107
  315.0 2.9 gather_fusion.11
  319.6 16.1 %psum.7 = f32[128]{0:T(128)S(1)} all-reduce(f32[128]{0:T(128)S(1)} %multiply_reduce_fusion.1), channel_id=1, replica_groups=mesh['tile'=64,'tm'=8] {'tm'}, use_global_device_ids=true, to_apply=%region_10.12 | all-reduce | flops 128 | bytes 1024 | tf_op jit(solution)/shard_map/psum | solution.py:79
  (86 shorter events, 21.2 us)
Async XLA Ops:
  0.6 28.6 %copy-start = (bf16[128,8,128]{2,1,0:T(8,128)(2,1)S(1)}, bf16[128,8,128]{2,1,0:T(8,128)(2,1)}, u32[]{:S(2)}) copy-start(bf16[128,8,128]{2,1,0:T(8,128)(2,1)} %param.18) | copy-start | bytes 786436
  0.6 26.1 %copy-start.2 = (s32[128,8]{0,1:T(8,128)S(1)}, s32[128,8]{0,1:T(8,128)}, u32[]{:S(2)}) copy-start(s32[128,8]{0,1:T(8,128)} %param.20) | copy-start | bytes 12292
  0.7 26.1 %copy-start.3 = (s32[1,64,8]{1,2,0:T(8,128)S(1)}, s32[1,64,8]{1,2,0:T(8,128)}, u32[]{:S(2)}) copy-start(s32[1,64,8]{1,2,0:T(8,128)} %param.19) | copy-start | bytes 6148
  0.7 26.3 %copy-start.1 = (bf16[128,8,128]{2,1,0:T(8,128)(2,1)S(1)}, bf16[128,8,128]{2,1,0:T(8,128)(2,1)}, u32[]{:S(2)}) copy-start(bf16[128,8,128]{2,1,0:T(8,128)(2,1)} %param.21) | copy-start | bytes 786436
  9.9 62.7 %all-to-all-start.1 = ((f32[64,1,1024]{2,1,0:T(1,128)}), f32[64,1,1024]{2,1,0:T(1,128)S(1)}, u32[]{:S(2)}, u32[]{:S(2)}) async-start(f32[64,1,1024]{2,1,0:T(1,128)} %reshape.406), calls=%async_computation.1 | async-start | bytes 524288 | tf_op jit(solution)/shard_map/all_to_all | solution.py:57
  72.7 35.6 %all-to-all-start = ((bf16[64,8,8,128]{3,2,1,0:T(8,128)(2,1)}), bf16[64,8,8,128]{3,2,1,0:T(8,128)(2,1)S(1)}, u32[]{:S(2)}, u32[]{:S(2)}) async-start(bf16[64,8,8,128]{3,2,1,0:T(8,128)(2,1)} %bitcast.2), calls=%async_computation | async-start | bytes 2097152 | tf_op jit(solution)/shard_map/all_to_all | solution.py:21
  265.6 52.4 %copy-start.4 = (f32[32]{0:T(128)S(1)}, f32[32]{0:T(128)}, u32[]{:S(2)}) copy-start(f32[32]{0:T(128)} %get-tuple-element.153) | copy-start | bytes 388
